TPU v7x, 256 devices: a whole 4x4x8 slice. The times are simulated.
256 devices in a mesh: grp: 8 (over z), sub: 32 (over x, y, core).
Axes of the slice: x: 4, y: 4, z: 8, core: 2. Of those that a mesh axis runs over, the one named last changes fastest.
Arguments:
- residual: float32 [16, 98304], P(None, 'sub'), may hold values from -6 to 6
- margin: int32 [32, 8], replicated, may hold values from 0 to 767, as said below
- aggregate: int32 [768], P('sub'), may hold values from 0 to 63
- local_factor: bfloat16 [32, 4096, 4096], P('sub', 'grp'), may hold values from -0.09375 to 0.09375
- coarse_factor: bfloat16 [8192, 8192], P('sub'), may hold values from -0.0625 to 0.0625
Outputs:
- preconditioned: float32 [16, 98304], P('grp', 'sub')
Inputs may be any that keep to these rules, and one draw needn't show every extreme that they name: `margin`: for subdomain s, every entry names a block owned by another subdomain (block b is owned by subdomain b // 24); the entries of one row are distinct. Up to 8 entries of one row may name blocks of the same owner, and in every draw some row takes all of its entries from a single owner. `aggregate`: the counts of global blocks for each coarse block are whole numbers and may cross devices as int32.
All inputs are finite; a program needn't handle non-finite values.
Results may differ from a plain program's by a relative error of at most 0.0033.
Values sent between devices are 32-bit elements; how exact they have to be, the bound alone decides.
A program may use at most 64 MiB of HBM per device.

v0:
```python
import jax
import jax.numpy as jnp
from jax import lax
from jax.sharding import PartitionSpec as P

BLK = 128
NCB = 64


def row_of(table, index):
    return lax.dynamic_index_in_dim(table, index, 0, keepdims=False)


def on_device(residual, margin, aggregate, local_factor, coarse_factor):
    sub_count = lax.axis_size("sub")
    grp_count = lax.axis_size("grp")
    my_index = lax.axis_index("sub")
    grp_index = lax.axis_index("grp")
    rhs_count, own_width = residual.shape
    owned = own_width // BLK
    group_rows = rhs_count // grp_count
    blocks = residual.reshape(rhs_count, owned, BLK)
    exact = lax.Precision.HIGHEST
    my_list = row_of(margin, my_index)
    all_blocks = jnp.arange(owned * sub_count, dtype=jnp.int32)
    selector = (my_list[:, None] == all_blocks[None, :]).astype(jnp.float32)
    whole = lax.all_gather(blocks, "sub", axis=1, tiled=True)
    halo_rows = jnp.einsum("kb,rbc->rkc", selector, whole, precision=exact)
    local_rhs = (
        jnp.concatenate([blocks, halo_rows], axis=1).reshape(rhs_count, -1).astype(jnp.bfloat16)
    )
    factor = local_factor[0]
    inner_term = jnp.dot(local_rhs, factor.T, preferred_element_type=jnp.float32).astype(
        jnp.bfloat16
    )
    local_sol = lax.psum_scatter(
        jnp.dot(inner_term, factor, preferred_element_type=jnp.float32),
        "grp",
        scatter_dimension=0,
        tiled=True,
    )
    local_sol = local_sol.reshape(group_rows, -1, BLK)
    own_part = local_sol[:, :owned]
    back_rows = local_sol[:, owned:]
    spread = jnp.einsum("kb,rkc->rbc", selector, back_rows, precision=exact)
    returned = lax.psum_scatter(spread, "sub", scatter_dimension=1, tiled=True)
    catalog = jnp.arange(NCB, dtype=jnp.int32)
    member = (aggregate[:, None] == catalog[None, :]).astype(jnp.float32)
    mine = lax.dynamic_slice_in_dim(blocks, grp_index * group_rows, group_rows, 0)
    sums_part = jnp.einsum("rbk,bj->rjk", mine, member, precision=exact)
    sums, counts = lax.psum((sums_part, jnp.sum(member, axis=0)), "sub")
    coarse_rhs = (
        (sums / jnp.maximum(counts, 1.0)[None, :, None])
        .reshape(group_rows, -1)
        .astype(jnp.bfloat16)
    )
    inner_coarse = jnp.dot(coarse_rhs, coarse_factor.T, preferred_element_type=jnp.float32).astype(
        jnp.bfloat16
    )
    coarse_part = jnp.dot(inner_coarse, coarse_factor, preferred_element_type=jnp.float32)
    coarse_sol = lax.psum(coarse_part, "sub")
    prolonged = jnp.einsum(
        "rjk,bj->rbk", coarse_sol.reshape(group_rows, NCB, BLK), member, precision=exact
    )
    result = own_part + returned + prolonged
    return result.reshape(group_rows, -1)


def solution(mesh):
    placed = (P(None, "sub"), P(), P("sub"), P("sub", "grp", None), P("sub", None))
    return jax.shard_map(
        on_device, mesh=mesh, in_specs=placed, out_specs=P("grp", "sub"), check_vma=False
    )
```

profile of v0, /device:TPU:2, one launch (start us, length us, event | category | flops | bytes accessed | tf_op | source)
XLA Modules:
  0.0 460.0 jit_solution(2734043562929597561)
XLA Ops:
  6.5 1.0 copy.9
  7.5 1.6 convolution_bitcast_fusion.2
  9.1 0.0 all-reduce.5.cloned.1.call-update
  9.2 0.0 all-gather.2.cloned.1.call-start
  9.2 0.7 all-gather.2.cloned.1.call-update
  9.9 0.0 all-reduce.9.cloned.1.call-start
  10.0 0.0 copy-done
  10.0 0.2 dynamic-slice_reduce_fusion
  10.2 1.3 dynamic-slice
  12.1 0.7 convert_reduce_fusion
  12.8 55.4 %psum.22 = f32[64]{0:T(128)S(1)} all-reduce(f32[64]{0:T(128)S(1)} %convert_reduce_fusion), channel_id=1, replica_groups=mesh['grp'=8,'sub'=32] {'sub'}, use_global_device_ids=true, to_apply=%region_4.5 | all-reduce | flops 64 | bytes 512 | tf_op jit(solution)/shard_map/psum | solution.py:51
  68.3 0.9 bitcast_convert_fusion
  69.2 50.8 %all-reduce.5.cloned.1.call-done = f32[2,64,128]{2,1,0:T(8,128)} async-done(((f32[2,64,128]{2,1,0:T(8,128)}), f32[2,64,128]{2,1,0:T(8,128)}) %all-reduce.5.cloned.1.call-update) | async-done | bytes 65552 | tf_op jit(solution)/shard_map/psum | solution.py:51
  120.0 0.9 fusion.20
  120.9 54.7 %all-gather.2.cloned.1.call-done = f32[16,768,128]{2,1,0:T(8,128)} async-done(((f32[16,24,128]{2,1,0:T(8,128)}), f32[16,768,128]{2,1,0:T(8,128)}) %all-gather.2.cloned.1.call-update) | async-done | bytes 6291472 | tf_op jit(solution)/shard_map/all_gather | solution.py:27
  175.7 4.8 %fusion.4 = bf16[16,8,128]{2,1,0:T(8,128)(2,1)S(1)} fusion(f32[16,768,128]{2,1,0:T(8,128)} %all-gather.2.cloned.1.call-done, s32[8]{0:T(128)S(1)} %dynamic-slice_reduce_fusion), kind=kOutput, calls=%fused_computation.8 | convolution fusion | flops 151017472 | bytes 6324256 | tf_op jit(solution)/shard_map/kb,rbc->rkc/dot_general | solution.py:28
  180.5 6.0 %fusion = f32[16,4096]{1,0:T(8,128)} fusion(bf16[1,512,4096]{2,1,0:T(8,128)(2,1)} %param.8, bf16[2,8,32,128]{3,2,1,0:T(8,128)(2,1)S(1)} %bitcast.65), kind=kOutput, calls=%fused_computation | convolution fusion | flops 134225920 | bytes 4587520 | tf_op jit(solution)/shard_map/dot_general | solution.py:37
  186.5 0.0 all-reduce.9.cloned.1.call-update
  186.5 0.0 copy-start.2
  186.6 0.0 all-reduce.7.cloned.1.call-start
  186.6 6.4 %convolution_bitcast_fusion.1 = f32[1,2,64,128]{3,1,2,0:T(2,128)S(1)} fusion(bf16[256,8192]{1,0:T(8,128)(2,1)} %param.9, bf16[1,2,64,128]{3,2,1,0:T(8,128)(2,1)S(1)} %fusion.20), kind=kOutput, calls=%fused_computation.5 | convolution fusion | flops 16777728 | bytes 4292608 | tf_op jit(solution)/shard_map/dot_general | solution.py:60
  193.0 0.6 copy.28
  193.6 0.0 all-reduce.7.cloned.1.call-update
  193.6 0.0 reduce-scatter.2.cloned.1.call-start
  193.7 65.8 %all-reduce.9.cloned.1.call-done = f32[16,4096]{1,0:T(8,128)} async-done(((f32[16,4096]{1,0:T(8,128)}), f32[16,4096]{1,0:T(8,128)}) %all-reduce.9.cloned.1.call-update) | async-done | bytes 262160
  259.4 0.9 dynamic-slice_bitcast_fusion
  260.4 1.5 convolution_bitcast_fusion
  261.8 0.0 reduce-scatter.2.cloned.1.call-update
  261.9 105.6 %all-reduce.7.cloned.1.call-done = f32[2,64,128]{2,1,0:T(8,128)} async-done(((f32[2,64,128]{2,1,0:T(8,128)}), f32[2,64,128]{2,1,0:T(8,128)}) %all-reduce.7.cloned.1.call-update) | async-done | bytes 65552 | tf_op jit(solution)/shard_map/psum | solution.py:61
  367.4 84.3 %reduce-scatter.2.cloned.1.call-done = f32[2,24,128]{2,1,0:T(8,128)} async-done(((f32[2,768,128]{2,1,0:T(8,128)}), f32[2,24,128]{2,1,0:T(8,128)}) %reduce-scatter.2.cloned.1.call-update) | async-done | bytes 24592 | tf_op jit(solution)/shard_map/reduce_scatter | solution.py:46
  451.8 1.0 fusion.11
  452.8 0.6 copy.30
  (8 shorter events, 0.0 us)
Async XLA Ops:
  6.5 3.5 copy-start
  6.5 113.4 %all-reduce.5.cloned.1.call-start = ((), (), s32[]{:S(2)}) async-start(), calls=%async_computation.3 | async-start | bytes 131072 | tf_op jit(solution)/shard_map/psum | solution.py:51
  7.5 1.7 copy-start.1
  9.2 166.5 %all-gather.2.cloned.1.call-start = ((), (), s32[]{:S(2)}) async-start(), calls=%async_computation.1 | async-start | bytes 6488064 | tf_op jit(solution)/shard_map/all_gather | solution.py:27
  9.9 249.5 %all-reduce.9.cloned.1.call-start = ((), (), s32[]{:S(2)}) async-start(), calls=%async_computation.5 | async-start | bytes 524288
  186.5 265.2 %copy-start.2 = (s32[24]{0:T(128)S(1)}, s32[24]{0:T(128)}, u32[]{:S(2)}) copy-start(s32[24]{0:T(128)} %param.7) | copy-start | bytes 292
  186.6 180.9 %all-reduce.7.cloned.1.call-start = ((), (), s32[]{:S(2)}) async-start(), calls=%async_computation.4 | async-start | bytes 131072 | tf_op jit(solution)/shard_map/psum | solution.py:61
  193.6 258.1 %reduce-scatter.2.cloned.1.call-start = ((), (), s32[]{:S(2)}) async-start(), calls=%async_computation.2 | async-start | bytes 811008 | tf_op jit(solution)/shard_map/reduce_scatter | solution.py:46
Sparse Core Ops, SparseCore 0:
  10.6 109.3 all-reduce.4
  122.7 52.9 all-gather.1
  186.7 72.7 all-reduce.8
  262.5 104.8 all-reduce.6
  371.1 80.6 reduce-scatter.1
where the time goes:
time: 460 us
  waiting for transfers between devices  362 us (79%)
  blocking collectives  55.4 us (12%)
  matrix products  21.3 us (5%)
  between operations  13.9 us (3%)
  local copies, waits for them, and re-layouts  4.62 us (1%)
    psum x1, waiting for transfers between devices, on_device(): coarse_sol = lax.psum(coarse_part, 'sub')  106 us
    reduce_scatter x1, waiting for transfers between devices, on_device(): returned = lax.psum_scatter(spread, 'sub', scatter_dimension=1, tiled=True)  84.3 us
    unnamed x6, waiting for transfers between devices  66.5 us
    psum x1, blocking collectives, on_device(): sums, counts = lax.psum((sums_part, jnp.sum(member, axis=0)), 'sub')  55.4 us
    all_gather x1, waiting for transfers between devices, on_device(): whole = lax.all_gather(blocks, 'sub', axis=1, tiled=True)  54.7 us
    psum x1, waiting for transfers between devices, on_device(): sums, counts = lax.psum((sums_part, jnp.sum(member, axis=0)), 'sub')  50.8 us
  transfers between devices with their start and end apart: 5, of which 5 were waited for; matrix products, arithmetic and copies ran while one was open for 3% of the time, Pallas kernels for 0%

commit v1 on v0

--- a/solution.py
+++ b/solution.py
@@ -24,7 +24,10 @@
     my_list = row_of(margin, my_index)
     all_blocks = jnp.arange(owned * sub_count, dtype=jnp.int32)
     selector = (my_list[:, None] == all_blocks[None, :]).astype(jnp.float32)
-    whole = lax.all_gather(blocks, "sub", axis=1, tiled=True)
+    count = lax.axis_size("sub")
+    pieces = jnp.stack([blocks for _ in range(count)])
+    pieces = lax.all_to_all(pieces, "sub", split_axis=0, concat_axis=0)
+    whole = jnp.concatenate(pieces, axis=1)
     halo_rows = jnp.einsum("kb,rbc->rkc", selector, whole, precision=exact)
     local_rhs = (
         jnp.concatenate([blocks, halo_rows], axis=1).reshape(rhs_count, -1).astype(jnp.bfloat16)

time: 460 us -> 374 us (0.81)
  waiting for transfers between devices: 362 us -> 193 us
  blocking collectives: 55.4 us -> 125 us
  starting transfers between devices: 0.17 us -> 7.98 us
  local copies, waits for them, and re-layouts: 4.62 us -> 10.7 us
    reduce_scatter x1, waiting for transfers between devices: 84.3 us -> 0.01 us  [on_device(): returned = lax.psum_scatter(spread, 'sub', scatter_dimension=1, tiled=True)]
    psum x1, blocking collectives: 55.4 us -> 125 us  [on_device(): sums, counts = lax.psum((sums_part, jnp.sum(member, axis=0)), 'sub')]
    all_gather x1 -> x0, waiting for transfers between devices: 54.7 us -> none  [on_device(): whole = lax.all_gather(blocks, 'sub', axis=1, tiled=True)]
    psum x1, waiting for transfers between devices: 50.8 us -> 22.3 us  [on_device(): sums, counts = lax.psum((sums_part, jnp.sum(member, axis=0)), 'sub')]
    all_to_all x0 -> x1, starting transfers between devices: none -> 7.81 us  [on_device(): pieces = lax.all_to_all(pieces, 'sub', split_axis=0, concat_axis=0)]
    unnamed x6 -> x5, waiting for transfers between devices: 66.5 us -> 65.6 us
  transfers between devices with their start and end apart: 5 -> 5, of which waited for: 5 -> 3; matrix products, arithmetic and copies ran while one was open for 3% -> 3% of each run, Pallas kernels for 0% -> 0%
where the time goes in v1:
time: 374 us; the launch traced here: 371 us
  waiting for transfers between devices  193 us (52%)
  blocking collectives  125 us (33%)
  matrix products  17.9 us (5%)
  between operations  15.6 us (4%)
  local copies, waits for them, and re-layouts  10.7 us (3%)
  starting transfers between devices  7.98 us (2%)
    psum x1, blocking collectives, on_device(): sums, counts = lax.psum((sums_part, jnp.sum(member, axis=0)), 'sub')  125 us
    psum x1, waiting for transfers between devices, on_device(): coarse_sol = lax.psum(coarse_part, 'sub')  105 us
    unnamed x5, waiting for transfers between devices  65.6 us
    psum x1, waiting for transfers between devices, on_device(): sums, counts = lax.psum((sums_part, jnp.sum(member, axis=0)), 'sub')  22.3 us
    all_to_all x1, starting transfers between devices, on_device(): pieces = lax.all_to_all(pieces, 'sub', split_axis=0, concat_axis=0)  7.81 us
  transfers between devices with their start and end apart: 5, of which 3 were waited for; matrix products, arithmetic and copies ran while one was open for 3% of the time, Pallas kernels for 0%

profile of v1, /device:TPU:2, one launch (start us, length us, event | category | flops | bytes accessed | tf_op | source)
XLA Modules:
  0.0 371.5 jit_solution(944263574681960436)
XLA Ops:
  7.4 0.0 copy-start
  7.4 1.0 copy.10
  8.4 3.4 stack.3
  11.7 7.8 %all-to-all-start = ((f32[32,16,24,128]{3,2,1,0:T(8,128)}), f32[32,16,24,128]{3,2,1,0:T(8,128)}, u32[]{:S(2)}, u32[]{:S(2)}) async-start(f32[32,16,24,128]{3,2,1,0:T(8,128)} %stack.3), calls=%async_computation | async-start | bytes 12582912 | tf_op jit(solution)/shard_map/all_to_all | solution.py:29
  19.5 0.0 all-reduce.5.cloned.1.call-start
  19.6 0.0 copy-done.1
  19.6 0.9 convolution_bitcast_fusion.2
  20.5 0.0 all-reduce.5.cloned.1.call-update
  20.5 0.0 all-reduce.9.cloned.1.call-start
  20.6 0.1 convert_reduce_fusion
  20.7 125.0 %psum.22 = f32[64]{0:T(128)S(1)} all-reduce(f32[64]{0:T(128)S(1)} %convert_reduce_fusion), channel_id=1, replica_groups=mesh['grp'=8,'sub'=32] {'sub'}, use_global_device_ids=true, to_apply=%region_4.5 | all-reduce | flops 64 | bytes 512 | tf_op jit(solution)/shard_map/psum | solution.py:54
  145.7 0.6 dynamic-slice
  146.9 0.2 dynamic-slice_reduce_fusion
  147.1 22.3 %all-reduce.5.cloned.1.call-done = f32[2,64,128]{2,1,0:T(8,128)} async-done(((f32[2,64,128]{2,1,0:T(8,128)}), f32[2,64,128]{2,1,0:T(8,128)}) %all-reduce.5.cloned.1.call-update) | async-done | bytes 65552 | tf_op jit(solution)/shard_map/psum | solution.py:54
  169.5 0.9 fusion.20
  170.4 0.0 all-to-all-done
  170.4 3.4 copy.7
  173.8 2.2 fusion.4
  176.0 6.0 %fusion = f32[16,4096]{1,0:T(8,128)} fusion(bf16[1,512,4096]{2,1,0:T(8,128)(2,1)} %param.8, bf16[2,8,32,128]{3,2,1,0:T(8,128)(2,1)S(1)} %bitcast.68), kind=kOutput, calls=%fused_computation | convolution fusion | flops 134225920 | bytes 4587520 | tf_op jit(solution)/shard_map/dot_general | solution.py:40
  182.0 0.0 all-reduce.9.cloned.1.call-update
  182.0 0.0 all-reduce.7.cloned.1.call-start
  182.1 6.4 %convolution_bitcast_fusion.1 = f32[1,2,64,128]{3,1,2,0:T(2,128)S(1)} fusion(bf16[256,8192]{1,0:T(8,128)(2,1)} %param.9, bf16[1,2,64,128]{3,2,1,0:T(8,128)(2,1)S(1)} %fusion.20), kind=kOutput, calls=%fused_computation.5 | convolution fusion | flops 16777728 | bytes 4292608 | tf_op jit(solution)/shard_map/dot_general | solution.py:63
  188.4 0.6 copy.29
  189.1 0.0 all-reduce.7.cloned.1.call-update
  189.1 0.0 reduce-scatter.2.cloned.1.call-start
  189.1 65.6 %all-reduce.9.cloned.1.call-done = f32[16,4096]{1,0:T(8,128)} async-done(((f32[16,4096]{1,0:T(8,128)}), f32[16,4096]{1,0:T(8,128)}) %all-reduce.9.cloned.1.call-update) | async-done | bytes 262160
  254.7 0.9 dynamic-slice_bitcast_fusion
  255.6 1.5 convolution_bitcast_fusion
  257.1 0.0 reduce-scatter.2.cloned.1.call-update
  257.1 105.2 %all-reduce.7.cloned.1.call-done = f32[2,64,128]{2,1,0:T(8,128)} async-done(((f32[2,64,128]{2,1,0:T(8,128)}), f32[2,64,128]{2,1,0:T(8,128)}) %all-reduce.7.cloned.1.call-update) | async-done | bytes 65552 | tf_op jit(solution)/shard_map/psum | solution.py:64
  362.4 1.0 fusion.11
  363.4 0.6 copy.31
  (9 shorter events, 0.0 us)
Async XLA Ops:
  7.4 139.6 %copy-start = (s32[32,8]{0,1:T(8,128)S(1)}, s32[32,8]{0,1:T(8,128)}, u32[]{:S(2)}) copy-start(s32[32,8]{0,1:T(8,128)} %param.6) | copy-start | bytes 3076
  11.7 7.9 %copy-start.1 = (s32[24]{0:T(128)S(1)}, s32[24]{0:T(128)}, u32[]{:S(2)}) copy-start(s32[24]{0:T(128)} %param.7) | copy-start | bytes 292
  11.7 134.0 %copy-start.2 = (u32[256]{0:T(256)S(1)}, u32[256]{0:T(256)}, u32[]{:S(2)}) copy-start(u32[256]{0:T(256)} %constant.28) | copy-start | bytes 3076
  11.7 158.7 %all-to-all-start = ((f32[32,16,24,128]{3,2,1,0:T(8,128)}), f32[32,16,24,128]{3,2,1,0:T(8,128)}, u32[]{:S(2)}, u32[]{:S(2)}) async-start(f32[32,16,24,128]{3,2,1,0:T(8,128)} %stack.3), calls=%async_computation | async-start | bytes 12582912 | tf_op jit(solution)/shard_map/all_to_all | solution.py:29
  19.5 149.9 %all-reduce.5.cloned.1.call-start = ((), (), s32[]{:S(2)}) async-start(), calls=%async_computation.3 | async-start | bytes 131072 | tf_op jit(solution)/shard_map/psum | solution.py:54
  20.5 234.2 %all-reduce.9.cloned.1.call-start = ((), (), s32[]{:S(2)}) async-start(), calls=%async_computation.5 | async-start | bytes 524288
  182.0 180.3 %all-reduce.7.cloned.1.call-start = ((), (), s32[]{:S(2)}) async-start(), calls=%async_computation.4 | async-start | bytes 131072 | tf_op jit(solution)/shard_map/psum | solution.py:64
  189.1 173.3 %reduce-scatter.2.cloned.1.call-start = ((), (), s32[]{:S(2)}) async-start(), calls=%async_computation.2 | async-start | bytes 811008 | tf_op jit(solution)/shard_map/reduce_scatter | solution.py:49
Sparse Core Ops, SparseCore 0:
  23.6 145.8 all-reduce.4
  257.3 79.3 reduce-scatter.1
Sparse Core Ops, SparseCore 1:
  182.1 72.5 all-reduce.8
  257.8 104.5 all-reduce.6
